TPU v7x, 512 devices: a whole 4x8x8 slice. The times are simulated.
512 devices in a mesh: section: 16 (over x_hi, z), expert: 32 (over x_lo, y, core).
Axes of the slice: x: 4 (x_hi: 2, x_lo: 2; x = x_hi * 2 + x_lo), y: 8, z: 8, core: 2. Of those that a mesh axis runs over, the one named last changes fastest.
Arguments:
- tokens: bfloat16 [4096, 6144], P('expert', 'section'), may hold values from -12 to 12
- route: int32 [4096, 2], P('expert'), may hold values from 0 to 7, all different within a row; in each aligned block of 128 rows (0 to 127, 128 to 255, ...) at most 40 rows name the same one
- norm_gain: float32 [6144], replicated, may hold values from 0.5 to 1.5
- router: bfloat16 [6144, 8], replicated, may hold values from -0.078125 to 0.078125
- gate_weight: bfloat16 [32, 16, 128, 6144], P('expert', 'section'), may hold values from -0.078125 to 0.078125
- up_weight: bfloat16 [32, 16, 128, 6144], P('expert', 'section'), may hold values from -0.078125 to 0.078125
Outputs:
- expert_hidden: bfloat16 [32, 32, 40, 16, 128], P('expert', None, None, 'section')
Inputs may be any that keep to these rules, and one draw needn't show every extreme that they name: `route`: among the 128 tokens of one index of expert no expert is named more than 40 times, and a token's two ids differ.
All inputs are finite; a program needn't handle non-finite values.
Results may differ from a plain program's by a relative error of at most 0.0065.
Values may be sent and summed in bfloat16 or wider, within the bound.
A program may use at most 64 MiB of HBM per device.

v0:
```python
import jax
import jax.numpy as jnp
from jax import lax
from jax.sharding import PartitionSpec as P

D = 6144


def place_rows(normed_part, logits, route, expert_count, capacity):
    one_hot = route[:, :, None] == jnp.arange(expert_count, dtype=jnp.int32)[None, None, :]
    picked = jnp.sum(jnp.where(one_hot, logits[:, None, :], jnp.float32(0.0)), axis=-1)
    weight_first = 1.0 / (1.0 + jnp.exp(picked[:, 1] - picked[:, 0]))
    weight_second = 1.0 / (1.0 + jnp.exp(picked[:, 0] - picked[:, 1]))
    pair_flat = jnp.stack([weight_first, weight_second], axis=1).astype(jnp.bfloat16).reshape(-1)
    flat_hot = one_hot.reshape(-1, expert_count).astype(jnp.int32)
    slot_rank = jnp.sum((jnp.cumsum(flat_hot, axis=0) - flat_hot) * flat_hot, axis=1)
    rank_hot = slot_rank[:, None] == jnp.arange(capacity, dtype=jnp.int32)[None, :]
    placing = ((flat_hot[:, :, None] > 0) & rank_hot[:, None, :]).reshape(
        flat_hot.shape[0], expert_count * capacity
    )
    doubled = jnp.repeat(normed_part, 2, axis=0)
    own_rows = jnp.einsum(
        "rs,rd->sd", placing.astype(jnp.bfloat16), doubled, preferred_element_type=jnp.float32
    )
    own_rows = own_rows.astype(jnp.bfloat16).reshape(expert_count, capacity, -1)
    own_weight = jnp.sum(
        jnp.where(placing, pair_flat.astype(jnp.float32)[:, None], jnp.float32(0.0)), axis=0
    )
    own_weight = own_weight.astype(jnp.bfloat16).reshape(expert_count, capacity)
    return (own_rows, own_weight)


def on_device(tokens, route, norm_gain, router, gate_weight, up_weight):
    slot_count = lax.axis_size("expert")
    expert_count = router.shape[1]
    group_size = slot_count // expert_count
    capacity = 5 * route.shape[0] // 16
    gate_local = gate_weight[0, 0]
    up_local = up_weight[0, 0]
    width_local = tokens.shape[1]
    start_local = lax.axis_index("section") * width_local
    as_float = tokens.astype(jnp.float32)
    square_total = lax.psum(jnp.sum(as_float * as_float, axis=-1), "section")
    mean_square = (square_total / D)[:, None]
    gain_local = lax.dynamic_slice_in_dim(norm_gain, start_local, width_local, 0)
    normed = (as_float * lax.rsqrt(mean_square + 1e-05) * gain_local).astype(jnp.bfloat16)
    router_local = lax.dynamic_slice_in_dim(router, start_local, width_local, 0)
    partial_logits = jnp.dot(normed, router_local, preferred_element_type=jnp.float32)
    logits = lax.psum(partial_logits, "section")
    own_rows, own_weight = place_rows(normed, logits, route, expert_count, capacity)
    sent_rows = jnp.repeat(own_rows, group_size, axis=0)
    sent_weight = jnp.repeat(own_weight, group_size, axis=0)
    recv_rows, recv_weight = (
        lax.all_to_all(sent_rows, "expert", split_axis=0, concat_axis=0, tiled=True),
        lax.all_to_all(sent_weight, "expert", split_axis=0, concat_axis=0, tiled=True),
    )
    piece = lax.all_gather(recv_rows, "section", axis=2, tiled=True)
    gate_next = jnp.einsum("scd,fd->scf", piece, gate_local, preferred_element_type=jnp.float32)
    up_next = jnp.einsum("scd,fd->scf", piece, up_local, preferred_element_type=jnp.float32)
    result = (jax.nn.silu(gate_next) * up_next * recv_weight.astype(jnp.float32)[..., None]).astype(
        jnp.bfloat16
    )
    return result[None, :, :, None, :]


def solution(mesh):
    in_specs = (
        P("expert", "section"),
        P("expert", None),
        P(),
        P(),
        P("expert", "section", None, None),
        P("expert", "section", None, None),
    )
    out_specs = P("expert", None, None, "section", None)
    return jax.shard_map(
        on_device, mesh=mesh, in_specs=in_specs, out_specs=out_specs, check_vma=False
    )
```

profile of v0, /device:TPU:1, one launch (start us, length us, event | category | flops | bytes accessed | tf_op | source)
XLA Modules:
  0.0 339.0 jit_solution(10291473496013722442)
XLA Ops:
  6.5 0.0 copy-start
  6.5 0.0 all-gather.2.cloned.1.call-start
  6.5 0.9 copy.28
  7.4 0.1 eq.53
  7.6 0.1 eq.57
  7.7 1.0 fusion.16
  8.7 41.7 %psum.14 = f32[128]{0:T(128)S(1)} all-reduce(f32[128]{0:T(128)S(1)} %fusion.16), channel_id=1, replica_groups=mesh['section'=16,'expert'=32] {'section'}, use_global_device_ids=true, to_apply=%region_4.5 | all-reduce | flops 128 | bytes 1024 | tf_op jit(solution)/shard_map/psum | solution.py:43
  50.5 0.6 reduce-window.6
  51.1 0.2 slice_reduce_fusion
  51.3 0.1 fusion.20
  51.4 0.8 dynamic_slice.6
  52.2 1.0 fusion.18
  53.2 0.1 broadcast_in_dim.47
  53.3 0.1 reshape.120
  53.4 0.3 convolution_convert_fusion
  53.7 0.1 broadcast_in_dim.48
  53.8 0.0 copy-start.1
  53.8 40.3 %all_to_all.14 = bf16[32,40,384]{2,1,0:T(8,128)(2,1)} all-to-all(bf16[32,40,384]{2,1,0:T(8,128)(2,1)S(1)} %bitcast.36), channel_id=1, replica_groups=mesh['section'=16,'expert'=32] {'expert'}, dimensions={0} | all-to-all | bytes 1966080 | tf_op jit(solution)/shard_map/all_to_all | solution.py:54
  94.1 0.0 all-gather.2.cloned.1.call-update
  94.1 0.8 fusion.22
  94.9 30.5 %psum.15 = f32[128,8]{0,1:T(8,128)S(1)} all-reduce(f32[128,8]{0,1:T(8,128)S(1)} %fusion.22), channel_id=1, replica_groups=mesh['section'=16,'expert'=32] {'section'}, use_global_device_ids=true, to_apply=%region_5.6 | all-reduce | flops 1024 | bytes 8192 | tf_op jit(solution)/shard_map/psum | solution.py:49
  125.4 0.0 copy-done.1
  125.5 0.1 copy.30
  125.6 0.1 reshape.123
  125.7 0.1 select_reduce_fusion
  125.9 20.7 %all_to_all.15 = bf16[32,1,40]{2,1,0:T(2,128)(2,1)S(1)} all-to-all(bf16[32,1,40]{2,1,0:T(2,128)(2,1)S(1)} %copy.31), channel_id=1, replica_groups=mesh['section'=16,'expert'=32] {'expert'}, dimensions={0} | all-to-all | bytes 5120 | tf_op jit(solution)/shard_map/all_to_all | solution.py:55
  146.6 0.0 copy-start.3
  146.6 170.1 %all-gather.2.cloned.1.call-done = bf16[32,40,6144]{2,1,0:T(8,128)(2,1)} async-done(((bf16[32,40,384]{2,1,0:T(8,128)(2,1)}), bf16[32,40,6144]{2,1,0:T(8,128)(2,1)}) %all-gather.2.cloned.1.call-update) | async-done | bytes 15728656 | tf_op jit(solution)/shard_map/all_gather | solution.py:57
  316.7 0.0 copy-done
  316.7 0.0 copy-start.2
  316.7 9.4 %fusion.2 = f32[32,40,128]{2,1,0:T(8,128)S(1)} fusion(bf16[32,40,6144]{2,1,0:T(8,128)(2,1)} %all-gather.2.cloned.1.call-done, bf16[1,1,128,6144]{3,2,1,0:T(8,128)(2,1)S(1)} %copy-done), kind=kOutput, calls=%fused_computation.2 | convolution fusion | flops 2013265920 | bytes 17956864 | tf_op jit(solution)/shard_map/scd,fd->scf/dot_general | solution.py:58
  326.1 0.0 copy-done.3
  326.1 0.5 copy-done.2
  326.7 5.5 %fusion.13 = bf16[1,32,40,1,128]{4,2,3,1,0:T(8,128)(2,1)} fusion(bf16[32,40,6144]{2,1,0:T(8,128)(2,1)S(1)} %copy-done.2, bf16[1,1,128,6144]{3,2,1,0:T(8,128)(2,1)S(1)} %copy-done.3, f32[32,40,128]{2,1,0:T(8,128)S(1)} %fusion.2, f32[32,40]{1,0:T(8,128)S(1)} %bitcast.40), kind=kOutput, calls=%fused_computation.8 | convolution fusion | flops 2014412800 | bytes 18289664 | tf_op jit(solution)/shard_map/scd,fd->scf/dot_general | solution.py:59
  (13 shorter events, 0.2 us)
Async XLA Ops:
  6.5 310.2 %copy-start = (bf16[1,1,128,6144]{3,2,1,0:T(8,128)(2,1)S(1)}, bf16[1,1,128,6144]{3,2,1,0:T(8,128)(2,1)}, u32[]{:S(2)}) copy-start(bf16[1,1,128,6144]{3,2,1,0:T(8,128)(2,1)} %param.10) | copy-start | bytes 4718596
  6.5 310.2 %all-gather.2.cloned.1.call-start = ((), (), s32[]{:S(2)}) async-start(), calls=%async_computation.2 | async-start | bytes 16711680 | tf_op jit(solution)/shard_map/all_gather | solution.py:57
  53.8 71.6 %copy-start.1 = (s32[128,2]{0,1:T(2,128)S(1)}, s32[128,2]{0,1:T(2,128)}, u32[]{:S(2)}) copy-start(s32[128,2]{0,1:T(2,128)} %param.7) | copy-start | bytes 3076
  146.6 179.5 %copy-start.3 = (bf16[1,1,128,6144]{3,2,1,0:T(8,128)(2,1)S(1)}, bf16[1,1,128,6144]{3,2,1,0:T(8,128)(2,1)}, u32[]{:S(2)}) copy-start(bf16[1,1,128,6144]{3,2,1,0:T(8,128)(2,1)} %param.11) | copy-start | bytes 4718596
  316.7 9.9 %copy-start.2 = (bf16[32,40,6144]{2,1,0:T(8,128)(2,1)S(1)}, bf16[32,40,6144]{2,1,0:T(8,128)(2,1)}, u32[]{:S(2)}) copy-start(bf16[32,40,6144]{2,1,0:T(8,128)(2,1)} %all-gather.2.cloned.1.call-done) | copy-start | bytes 47185924
Sparse Core Ops, SparseCore 0:
  94.2 222.4 all-gather.1
where the time goes:
time: 342 us; the launch traced here: 339 us
  waiting for transfers between devices  170 us (50%)
  blocking collectives  133 us (39%)
  matrix products  16 us (5%)
  between operations  13.5 us (4%)
    all_gather x1, waiting for transfers between devices, on_device(): piece = lax.all_gather(recv_rows, 'section', axis=2, tiled=True)  170 us
    psum x1, blocking collectives, on_device(): square_total = lax.psum(jnp.sum(as_float * as_float, axis=-1), 'section')  41.7 us
    all_to_all x1, blocking collectives, on_device(): lax.all_to_all(sent_rows, 'expert', split_axis=0, concat_axis=0, tiled=True)  40.3 us
    psum x1, blocking collectives, on_device(): logits = lax.psum(partial_logits, 'section')  30.5 us
    all_to_all x1, blocking collectives, on_device(): lax.all_to_all(sent_weight, 'expert', split_axis=0, concat_axis=0, tiled=...  20.7 us
    dot_general x1, matrix products, on_device(): jnp.einsum('scd,fd->scf', piece, gate_local, preferred_element_type=jnp.f...  9.39 us
  transfers between devices with their start and end apart: 1, of which 1 were waited for; matrix products, arithmetic and copies ran while one was open for 0% of the time, Pallas kernels for 0%

commit v1 on v0

v1 whole, which is shorter than its diff:
```python
import jax
import jax.numpy as jnp
from jax import lax
from jax.experimental import pallas as pl
from jax.experimental.pallas import tpu as pltpu
from jax.sharding import PartitionSpec as P

D = 6144
Z = 8
ROWS = 640
WIDTH = 384
EARLY = 448
COPIES = 80


def gather_matmul(own_ref, stat_ref, gate_ref, up_ref, acc_ref, tot_ref, full, stats, send, recv, local):
    sec = lax.axis_index("section")
    exp = lax.axis_index("expert")
    plane, z = sec // Z, lax.rem(sec, Z)
    core = lax.rem(exp, 2)
    up_sec = plane * Z + lax.rem(z + 1, Z)
    down_sec = plane * Z + lax.rem(z + Z - 1, Z)
    across_sec = (1 - plane) * Z + z
    peers = dict(
        up=(up_sec, exp),
        down=(down_sec, exp),
        across=(across_sec, exp),
        partner=(sec, exp + 1 - 2 * core),
    )
    barrier = pltpu.get_barrier_semaphore()
    for peer in peers.values():
        pl.semaphore_signal(barrier, inc=1, device_id=peer, device_id_type=pl.DeviceIdType.MESH)
    pl.semaphore_wait(barrier, len(peers))

    shift = (0, Z - 1, Z - 2, Z - 3, 1, 2, 3, 4)

    def mine(i):
        return plane * Z + lax.rem(z + shift[i], Z)

    def other(i):
        return (1 - plane) * Z + lax.rem(z + shift[i], Z)

    made = {}

    def start(name, peer, src, dst):
        n = len(made)
        copy = pltpu.make_async_remote_copy(
            src_ref=src,
            dst_ref=dst,
            send_sem=send.at[n],
            recv_sem=recv.at[n],
            device_id=peers[peer],
            device_id_type=pl.DeviceIdType.MESH,
        )
        copy.start()
        made[name] = copy

    def rows(i_sec, lo, n):
        return full.at[i_sec, core, pl.ds(lo, n)]

    early, late = (0, EARLY), (EARLY, ROWS - EARLY)

    def ring(kind, i, way, hop):
        n = ROWS if kind == 0 else EARLY
        lo = 0
        if hop == 4:
            n = n // 2
            lo = 0 if way == "up" else n
        dst = rows(mine(i) if kind == 0 else other(i), lo, n)
        src = own_ref.at[pl.ds(lo, n)] if (kind == 0 and i == 0) else dst
        start(("ring", kind, way, hop), way, src, dst)

    def ring_stat(i, way, hop):
        dst = stats.at[mine(i), core]
        start(("stat", way, hop), way, stat_ref if i == 0 else dst, dst)

    def spread(i):
        dst = rows(mine(i), *late)
        start(("late", i), "across", own_ref.at[pl.ds(*late)] if i == 0 else dst, dst)
        dst = stats.at[mine(i), core]
        src = stat_ref if i == 0 else dst
        start(("sx", i), "across", src, dst)
        start(("ps", i), "partner", src, dst)
        dst = rows(mine(i), 0, ROWS)
        start(("p0", i), "partner", own_ref if i == 0 else dst, dst)

    def spread_early(i):
        dst = rows(other(i), *early)
        start(("pe", i), "partner", dst, dst)

    def spread_late(i):
        made[("late", i)].wait_recv()
        made[("sx", i)].wait_recv()
        dst = rows(other(i), *late)
        start(("pl", i), "partner", dst, dst)
        dst = stats.at[other(i), core]
        start(("po", i), "partner", dst, dst)

    def multiply(s, first):
        cols = pl.ds(pl.multiple_of(s * WIDTH, 128), WIDTH)
        weights = jnp.concatenate([gate_ref[:, cols], up_ref[:, cols]], axis=0)

        @pl.loop(0, 4)
        def _(t):
            at = pl.ds(pl.multiple_of(lax.rem(t, 2) * 320, 32), 320)
            to = pl.ds(pl.multiple_of(t * 320, 32), 320)
            part = lax.dot_general(
                full[s, t // 2, at, :], weights, (((1,), (1,)), ((), ())),
                preferred_element_type=jnp.float32,
            )
            if first:
                acc_ref[to, :] = part
            else:
                acc_ref[to, :] += part

    def consume(i):
        made[("p0", i)].wait_recv()
        multiply(mine(i), i == 0)
        made[("pe", i)].wait_recv()
        made[("pl", i)].wait_recv()
        multiply(other(i), False)

    dst = rows(other(0), *early)
    start(("early",), "across", own_ref.at[pl.ds(*early)], rows(sec, *early))
    ring(0, 0, "up", 1)
    ring(0, 0, "down", 1)
    ring_stat(0, "up", 1)
    ring_stat(0, "down", 1)
    spread(0)
    keep = pltpu.make_async_copy(own_ref, full.at[sec, core], local.at[0])
    keep.start()
    keep_stat = pltpu.make_async_copy(stat_ref, stats.at[sec, core], local.at[1])
    keep_stat.start()
    made[("early",)].wait_recv()
    ring(1, 0, "up", 1)
    ring(1, 0, "down", 1)
    spread_early(0)
    keep.wait()
    keep_stat.wait()
    ways = (("up", 0), ("down", 3))
    for hop in (1, 2, 3):
        for way, base in ways:
            made[("ring", 0, way, hop)].wait_recv()
            ring(0, base + hop, way, hop + 1)
            made[("stat", way, hop)].wait_recv()
            if hop < 3 or way == "up":
                ring_stat(base + hop, way, hop + 1)
            spread(base + hop)
        for way, base in ways:
            made[("ring", 1, way, hop)].wait_recv()
            ring(1, base + hop, way, hop + 1)
            spread_early(base + hop)
        before = [0] if hop == 1 else [hop - 1, hop + 2]
        for i in before:
            spread_late(i)
        for i in before:
            consume(i)
    for way, _ in ways:
        made[("ring", 0, way, 4)].wait_recv()
    made[("stat", "up", 4)].wait_recv()
    spread(7)
    for way, _ in ways:
        made[("ring", 1, way, 4)].wait_recv()
    spread_early(7)
    for i in (3, 6):
        spread_late(i)
    for i in (3, 6):
        consume(i)
    spread_late(7)
    consume(7)
    for i in range(8):
        made[("ps", i)].wait_recv()
        made[("po", i)].wait_recv()
    tot_ref[...] = jnp.sum(stats[...], axis=0)
    for copy in made.values():
        copy.wait_send()


def place_rows(scaled, square_part, logit_part, route, expert_count, capacity):
    one_hot = route[:, :, None] == jnp.arange(expert_count, dtype=jnp.int32)[None, None, :]
    picked = jnp.sum(jnp.where(one_hot, logit_part[:, None, :], jnp.float32(0.0)), axis=-1)
    lead = jnp.stack([picked[:, 1] - picked[:, 0], picked[:, 0] - picked[:, 1]], axis=1).reshape(-1)
    square = jnp.repeat(square_part, 2)
    flat_hot = one_hot.reshape(-1, expert_count).astype(jnp.int32)
    slot_rank = jnp.sum((jnp.cumsum(flat_hot, axis=0) - flat_hot) * flat_hot, axis=1)
    rank_hot = slot_rank[:, None] == jnp.arange(capacity, dtype=jnp.int32)[None, :]
    placing = ((flat_hot[:, :, None] > 0) & rank_hot[:, None, :]).reshape(
        flat_hot.shape[0], expert_count * capacity
    )
    doubled = jnp.repeat(scaled, 2, axis=0)
    own_rows = jnp.einsum(
        "rs,rd->sd", placing.astype(jnp.bfloat16), doubled, preferred_element_type=jnp.float32
    ).astype(jnp.bfloat16)
    own_square = jnp.sum(jnp.where(placing, square[:, None], jnp.float32(0.0)), axis=0)
    own_lead = jnp.sum(jnp.where(placing, lead[:, None], jnp.float32(0.0)), axis=0)
    return own_rows, own_square, own_lead


def on_device(tokens, route, norm_gain, router, gate_weight, up_weight):
    expert_count, capacity = router.shape[1], 5 * route.shape[0] // 16
    half = capacity // 2
    slots = lax.axis_size("expert")
    start_local = lax.axis_index("section") * WIDTH
    as_float = tokens.astype(jnp.float32)
    square_part = jnp.sum(as_float * as_float, axis=-1)
    gain_local = lax.dynamic_slice_in_dim(norm_gain, start_local, WIDTH, 0)
    scaled = (as_float * gain_local).astype(jnp.bfloat16)
    router_local = lax.dynamic_slice_in_dim(router, start_local, WIDTH, 0)
    logit_part = jnp.dot(scaled, router_local, preferred_element_type=jnp.float32)
    own_rows, own_square, own_lead = place_rows(
        scaled, square_part, logit_part, route, expert_count, capacity
    )

    def to_slots(a, tail):
        a = a.reshape((expert_count, 1, 2) + tail)
        return jnp.broadcast_to(a, (expert_count, 2, 2) + tail).reshape((slots,) + tail)

    sent_rows = to_slots(own_rows, (half, WIDTH))
    sent_stat = jnp.stack(
        [to_slots(own_square, (half,)), to_slots(own_lead, (half,))], axis=1
    )
    recv_rows, recv_stat = (
        lax.all_to_all(sent_rows, "expert", split_axis=0, concat_axis=0, tiled=True),
        lax.all_to_all(sent_stat, "expert", split_axis=0, concat_axis=0, tiled=True),
    )
    stat = jnp.transpose(recv_stat, (1, 0, 2)).reshape(2, ROWS)
    stat = jnp.concatenate([stat, jnp.zeros((6, ROWS), jnp.float32)], axis=0)
    vmem = pl.BlockSpec(memory_space=pltpu.VMEM)
    acc, total = pl.pallas_call(
        gather_matmul,
        out_shape=(
            jax.ShapeDtypeStruct((2 * ROWS, 256), jnp.float32),
            jax.ShapeDtypeStruct((2, 8, ROWS), jnp.float32),
        ),
        in_specs=[vmem] * 4,
        out_specs=(vmem, vmem),
        scratch_shapes=[
            pltpu.VMEM((2 * Z, 2, ROWS, WIDTH), jnp.bfloat16),
            pltpu.VMEM((2 * Z, 2, 8, ROWS), jnp.float32),
            pltpu.SemaphoreType.DMA((COPIES,)),
            pltpu.SemaphoreType.DMA((COPIES,)),
            pltpu.SemaphoreType.DMA((2,)),
        ],
        compiler_params=pltpu.CompilerParams(
            collective_id=0, has_side_effects=True, vmem_limit_bytes=48 * 1024 * 1024
        ),
    )(recv_rows.reshape(ROWS, WIDTH), stat, gate_weight[0, 0], up_weight[0, 0])
    scale = lax.rsqrt(total[:, 0] / D + 1e-05)
    weight = (1.0 / (1.0 + jnp.exp(total[:, 1] * scale))).astype(jnp.bfloat16).astype(jnp.float32)
    acc = acc.reshape(2, slots, half, 256)
    scale = scale.reshape(2, slots, half, 1)
    weight = weight.reshape(2, slots, half, 1)
    result = jax.nn.silu(acc[..., :128] * scale) * (acc[..., 128:] * scale) * weight
    result = jnp.transpose(result.astype(jnp.bfloat16), (1, 0, 2, 3)).reshape(slots, capacity, 128)
    return result[None, :, :, None, :]


def solution(mesh):
    in_specs = (
        P("expert", "section"),
        P("expert", None),
        P(),
        P(),
        P("expert", "section", None, None),
        P("expert", "section", None, None),
    )
    out_specs = P("expert", None, None, "section", None)
    return jax.shard_map(
        on_device, mesh=mesh, in_specs=in_specs, out_specs=out_specs, check_vma=False
    )
```

time: 342 us -> 137 us (0.40)
  waiting for transfers between devices: 170 us -> 25.2 us
  blocking collectives: 133 us -> 0 us
  Pallas kernels: 0 us -> 85.8 us
  matrix products: 16 us -> 0.39 us
  starting transfers between devices: 0.01 us -> 14.8 us
  between operations: 13.5 us -> 0.22 us
  local copies, waits for them, and re-layouts: 3.27 us -> 6.69 us
    all_gather x1 -> x0, waiting for transfers between devices: 170 us -> none  [on_device(): piece = lax.all_gather(recv_rows, 'section', axis=2, tiled=True)]
    pallas_call x0 -> x1, Pallas kernels: none -> 85.8 us  [on_device(): pl.pallas_call(gather_matmul, out_shape=(jax.ShapeDtypeStruct((2 * ROWS,...]
    psum x2 -> x0, blocking collectives: 72.2 us -> none  [the longest x1 41.7 us: on_device(): square_total = lax.psum(jnp.sum(as_float * as_float, axis=-1), 'section')]
    all_to_all x2 -> x0, blocking collectives: 61 us -> none  [the longest x1 40.3 us: on_device(): lax.all_to_all(sent_rows, 'expert', split_axis=0, concat_axis=0, tiled=True)]
    all_to_all x0 -> x2, waiting for transfers between devices: none -> 25.2 us  [the longest x1 17.7 us: on_device(): lax.all_to_all(sent_rows, 'expert', split_axis=0, concat_axis=0, tiled=True)]
    dot_general x3 -> x1, matrix products: 15.8 us -> 0.13 us  [on_device(): jnp.dot(scaled, router_local, preferred_element_type=jnp.float32)]
    all_to_all x0 -> x2, starting transfers between devices: none -> 14.8 us  [the longest x1 10.3 us: on_device(): lax.all_to_all(sent_stat, 'expert', split_axis=0, concat_axis=0, tiled=True)]
  transfers between devices with their start and end apart: 1 -> 2, of which waited for: 1 -> 2; matrix products, arithmetic and copies ran while one was open for 0% -> 0% of each run, Pallas kernels for 0% -> 0%
where the time goes in v1:
time: 137 us
  Pallas kernels  85.8 us (63%)
  waiting for transfers between devices  25.2 us (18%)
  starting transfers between devices  14.8 us (11%)
  local copies, waits for them, and re-layouts  6.69 us (5%)
  other arithmetic  3.91 us (3%)
    pallas_call x1, Pallas kernels, on_device(): pl.pallas_call(gather_matmul, out_shape=(jax.ShapeDtypeStruct((2 * ROWS,...  85.8 us
    all_to_all x1, waiting for transfers between devices, on_device(): lax.all_to_all(sent_rows, 'expert', split_axis=0, concat_axis=0, tiled=True)  17.7 us
    all_to_all x1, starting transfers between devices, on_device(): lax.all_to_all(sent_stat, 'expert', split_axis=0, concat_axis=0, tiled=True)  10.3 us
    all_to_all x1, waiting for transfers between devices, on_device(): lax.all_to_all(sent_stat, 'expert', split_axis=0, concat_axis=0, tiled=True)  7.45 us
    all_to_all x1, starting transfers between devices, on_device(): lax.all_to_all(sent_rows, 'expert', split_axis=0, concat_axis=0, tiled=True)  4.45 us
  transfers between devices with their start and end apart: 2, of which 2 were waited for; matrix products, arithmetic and copies ran while one was open for 0% of the time, Pallas kernels for 0%

profile of v1, /device:TPU:1, one launch (start us, length us, event | category | flops | bytes accessed | tf_op | source)
XLA Modules:
  0.0 137.0 jit_solution(17932438275988349320)
XLA Ops:
  0.0 0.0 copy-start
  0.0 0.8 copy.24
  0.8 0.1 eq.57
  1.0 0.1 eq.53
  1.1 0.8 dynamic_slice.6
  1.9 1.0 fusion.5
  2.9 0.0 copy-done
  2.9 0.1 fusion.10
  3.0 0.7 select_reduce_fusion.2
  3.8 0.1 copy.26
  3.9 0.1 broadcast_in_dim.81
  4.0 0.1 broadcast_in_dim.73
  4.1 0.2 broadcast_in_dim.74
  4.3 0.6 reduce-window.6
  4.9 0.2 slice_reduce_fusion
  5.1 0.1 fusion.8
  5.2 0.2 select_reduce_fusion.1
  5.4 0.1 broadcast_in_dim.77
  5.5 0.1 broadcast_in_dim.83
  5.6 0.7 pad_maximum_fusion
  6.3 10.3 %all-to-all-start.1 = ((f32[32,2,20]{2,1,0:T(2,128)}), f32[32,2,20]{2,1,0:T(2,128)S(1)}, u32[]{:S(2)}, u32[]{:S(2)}) async-start(f32[32,2,20]{2,1,0:T(2,128)} %pad_maximum_fusion), calls=%async_computation.1 | async-start | bytes 65536 | tf_op jit(solution)/shard_map/all_to_all | solution.py:224
  16.7 0.1 broadcast_in_dim.70
  16.8 0.1 reshape.141
  16.8 0.3 convolution_convert_fusion
  17.1 0.1 broadcast_in_dim.71
  17.2 0.0 copy-start.1
  17.2 7.5 %all-to-all-done.1 = f32[32,2,20]{2,1,0:T(2,128)S(1)} async-done(((f32[32,2,20]{2,1,0:T(2,128)}), f32[32,2,20]{2,1,0:T(2,128)S(1)}, u32[]{:S(2)}, u32[]{:S(2)}) %all-to-all-start.1) | async-done | bytes 5152 | tf_op jit(solution)/shard_map/all_to_all | solution.py:224
  24.6 0.9 broadcast_in_dim.72
  25.5 4.5 %all-to-all-start = ((bf16[32,20,384]{2,1,0:T(8,128)(2,1)}), bf16[32,20,384]{2,1,0:T(8,128)(2,1)S(1)}, u32[]{:S(2)}, u32[]{:S(2)}) async-start(bf16[32,20,384]{2,1,0:T(8,128)(2,1)} %bitcast.3), calls=%async_computation | async-start | bytes 1179648 | tf_op jit(solution)/shard_map/all_to_all | solution.py:223
  30.0 0.1 reshape.144
  30.1 17.7 %all-to-all-done = bf16[32,20,384]{2,1,0:T(8,128)(2,1)S(1)} async-done(((bf16[32,20,384]{2,1,0:T(8,128)(2,1)}), bf16[32,20,384]{2,1,0:T(8,128)(2,1)S(1)}, u32[]{:S(2)}, u32[]{:S(2)}) %all-to-all-start) | async-done | bytes 491552 | tf_op jit(solution)/shard_map/all_to_all | solution.py:223
  47.8 0.1 reshape.143.own_ref
  47.9 0.0 copy-done.1
  47.9 0.0 copy-start.2
  47.9 1.4 %copy-done.2 = bf16[1,1,128,6144]{3,2,1,0:T(8,128)(2,1)S(1)} copy-done((bf16[1,1,128,6144]{3,2,1,0:T(8,128)(2,1)S(1)}, bf16[1,1,128,6144]{3,2,1,0:T(8,128)(2,1)}, u32[]{:S(2)}) %copy-start.2) | copy-done | bytes 1572888
  49.3 85.8 %shard_map.64 = (f32[1280,256]{1,0:T(8,128)S(1)}, f32[2,8,640]{2,1,0:T(8,128)S(1)}) custom-call(bf16[640,384]{1,0:T(8,128)(2,1)S(1)} %reshape.143.own_ref, f32[8,640]{1,0:T(8,128)S(1)} %concatenate.3.stat_ref, bf16[128,6144]{1,0:T(8,128)(2,1)S(1)} %bitcast.17, bf16[128,6144]{1,0:T(8,128)(2,1)S(1)} %bitcast.18), custom_call_target="tpu_custom_call" | custom-call | tf_op jit(solution)/shard_map/pallas_call | solution.py:229
  135.2 0.1 reshape.145
  135.4 0.1 rsqrt.14
  135.5 0.1 squeeze.16
  135.6 0.5 fusion.3
  136.2 0.9 copy.29
  (15 shorter events, 0.3 us)
Async XLA Ops:
  0.0 2.9 %copy-start = (bf16[6144,8]{0,1:T(8,128)(2,1)S(1)}, bf16[6144,8]{0,1:T(8,128)(2,1)}, u32[]{:S(2)}) copy-start(bf16[6144,8]{0,1:T(8,128)(2,1)} %param.9) | copy-start | bytes 294916
  6.3 18.4 %all-to-all-start.1 = ((f32[32,2,20]{2,1,0:T(2,128)}), f32[32,2,20]{2,1,0:T(2,128)S(1)}, u32[]{:S(2)}, u32[]{:S(2)}) async-start(f32[32,2,20]{2,1,0:T(2,128)} %pad_maximum_fusion), calls=%async_computation.1 | async-start | bytes 65536 | tf_op jit(solution)/shard_map/all_to_all | solution.py:224
  17.2 30.8 %copy-start.1 = (bf16[1,1,128,6144]{3,2,1,0:T(8,128)(2,1)S(1)}, bf16[1,1,128,6144]{3,2,1,0:T(8,128)(2,1)}, u32[]{:S(2)}) copy-start(bf16[1,1,128,6144]{3,2,1,0:T(8,128)(2,1)} %param.10) | copy-start | bytes 4718596
  25.5 22.3 %all-to-all-start = ((bf16[32,20,384]{2,1,0:T(8,128)(2,1)}), bf16[32,20,384]{2,1,0:T(8,128)(2,1)S(1)}, u32[]{:S(2)}, u32[]{:S(2)}) async-start(bf16[32,20,384]{2,1,0:T(8,128)(2,1)} %bitcast.3), calls=%async_computation | async-start | bytes 1179648 | tf_op jit(solution)/shard_map/all_to_all | solution.py:223
  47.9 1.4 %copy-start.2 = (bf16[1,1,128,6144]{3,2,1,0:T(8,128)(2,1)S(1)}, bf16[1,1,128,6144]{3,2,1,0:T(8,128)(2,1)}, u32[]{:S(2)}) copy-start(bf16[1,1,128,6144]{3,2,1,0:T(8,128)(2,1)} %param.11) | copy-start | bytes 4718596

commit v2 on v1

--- a/solution.py
+++ b/solution.py
@@ -9,8 +9,9 @@
 Z = 8
 ROWS = 640
 WIDTH = 384
-EARLY = 448
-COPIES = 80
+SPLIT = 208
+MIDDLE = ROWS - 2 * SPLIT
+COPIES = 86
 
 
 def gather_matmul(own_ref, stat_ref, gate_ref, up_ref, acc_ref, tot_ref, full, stats, send, recv, local):
@@ -18,6 +19,7 @@
     exp = lax.axis_index("expert")
     plane, z = sec // Z, lax.rem(sec, Z)
     core = lax.rem(exp, 2)
+    odd = lax.rem(exp // 2, 2)
     up_sec = plane * Z + lax.rem(z + 1, Z)
     down_sec = plane * Z + lax.rem(z + Z - 1, Z)
     across_sec = (1 - plane) * Z + z
@@ -26,6 +28,7 @@
         down=(down_sec, exp),
         across=(across_sec, exp),
         partner=(sec, exp + 1 - 2 * core),
+        side=(sec, exp + 2 - 4 * odd),
     )
     barrier = pltpu.get_barrier_semaphore()
     for peer in peers.values():
@@ -56,43 +59,54 @@
         made[name] = copy
 
     def rows(i_sec, lo, n):
-        return full.at[i_sec, core, pl.ds(lo, n)]
-
-    early, late = (0, EARLY), (EARLY, ROWS - EARLY)
+        return full.at[i_sec, core, pl.ds(pl.multiple_of(lo, 16), n)]
+
+    def own_rows(lo, n):
+        return own_ref.at[pl.ds(pl.multiple_of(lo, 16), n)]
+
+    kept = (odd * (ROWS - SPLIT), SPLIT)
+    rest = ((1 - odd) * SPLIT, ROWS - SPLIT)
+    middle = (SPLIT, MIDDLE)
 
     def ring(kind, i, way, hop):
-        n = ROWS if kind == 0 else EARLY
-        lo = 0
+        lo, n = (odd * SPLIT, SPLIT + MIDDLE) if kind == 0 else kept
         if hop == 4:
-            n = n // 2
-            lo = 0 if way == "up" else n
+            first = MIDDLE if kind == 0 else SPLIT // 2 + 8
+            lo, n = (lo, first) if way == "up" else (lo + first, n - first)
         dst = rows(mine(i) if kind == 0 else other(i), lo, n)
-        src = own_ref.at[pl.ds(lo, n)] if (kind == 0 and i == 0) else dst
-        start(("ring", kind, way, hop), way, src, dst)
+        start(("ring", kind, way, hop), way, own_rows(lo, n) if kind == 0 and i == 0 else dst, dst)
 
     def ring_stat(i, way, hop):
         dst = stats.at[mine(i), core]
         start(("stat", way, hop), way, stat_ref if i == 0 else dst, dst)
 
     def spread(i):
-        dst = rows(mine(i), *late)
-        start(("late", i), "across", own_ref.at[pl.ds(*late)] if i == 0 else dst, dst)
+        if i:
+            dst = rows(mine(i), *middle)
+            start(("late", i), "across", dst, dst)
+            dst = rows(mine(i), *kept)
+            start(("y0", i), "side", dst, dst)
         dst = stats.at[mine(i), core]
         src = stat_ref if i == 0 else dst
         start(("sx", i), "across", src, dst)
         start(("ps", i), "partner", src, dst)
-        dst = rows(mine(i), 0, ROWS)
-        start(("p0", i), "partner", own_ref if i == 0 else dst, dst)
-
-    def spread_early(i):
-        dst = rows(other(i), *early)
-        start(("pe", i), "partner", dst, dst)
-
-    def spread_late(i):
-        made[("late", i)].wait_recv()
+
+    def spread_other(i):
+        dst = rows(other(i), *kept)
+        start(("y1", i), "side", dst, dst)
+
+    def whole(i):
+        if i:
+            made[("y0", i)].wait_recv()
+            dst = rows(mine(i), 0, ROWS)
+            start(("p0", i), "partner", dst, dst)
+            made[("late", i)].wait_recv()
+            made[("y1", i)].wait_recv()
+        else:
+            made[("rest",)].wait_recv()
+        dst = rows(other(i), 0, ROWS)
+        start(("p1", i), "partner", dst, dst)
         made[("sx", i)].wait_recv()
-        dst = rows(other(i), *late)
-        start(("pl", i), "partner", dst, dst)
         dst = stats.at[other(i), core]
         start(("po", i), "partner", dst, dst)
 
@@ -116,25 +130,24 @@
     def consume(i):
         made[("p0", i)].wait_recv()
         multiply(mine(i), i == 0)
-        made[("pe", i)].wait_recv()
-        made[("pl", i)].wait_recv()
+        made[("p1", i)].wait_recv()
         multiply(other(i), False)
 
-    dst = rows(other(0), *early)
-    start(("early",), "across", own_ref.at[pl.ds(*early)], rows(sec, *early))
+    start(("kept",), "across", own_rows(*kept), rows(sec, *kept))
     ring(0, 0, "up", 1)
     ring(0, 0, "down", 1)
     ring_stat(0, "up", 1)
     ring_stat(0, "down", 1)
+    start(("rest",), "across", own_rows(*rest), rows(sec, *rest))
+    start(("p0", 0), "partner", own_ref, rows(sec, 0, ROWS))
     spread(0)
     keep = pltpu.make_async_copy(own_ref, full.at[sec, core], local.at[0])
     keep.start()
     keep_stat = pltpu.make_async_copy(stat_ref, stats.at[sec, core], local.at[1])
     keep_stat.start()
-    made[("early",)].wait_recv()
+    made[("kept",)].wait_recv()
     ring(1, 0, "up", 1)
     ring(1, 0, "down", 1)
-    spread_early(0)
     keep.wait()
     keep_stat.wait()
     ways = (("up", 0), ("down", 3))
@@ -149,10 +162,10 @@
         for way, base in ways:
             made[("ring", 1, way, hop)].wait_recv()
             ring(1, base + hop, way, hop + 1)
-            spread_early(base + hop)
+            spread_other(base + hop)
         before = [0] if hop == 1 else [hop - 1, hop + 2]
         for i in before:
-            spread_late(i)
+            whole(i)
         for i in before:
             consume(i)
     for way, _ in ways:
@@ -161,12 +174,12 @@
     spread(7)
     for way, _ in ways:
         made[("ring", 1, way, 4)].wait_recv()
-    spread_early(7)
+    spread_other(7)
     for i in (3, 6):
-        spread_late(i)
+        whole(i)
     for i in (3, 6):
         consume(i)
-    spread_late(7)
+    whole(7)
     consume(7)
     for i in range(8):
         made[("ps", i)].wait_recv()
@@ -215,15 +228,21 @@
         a = a.reshape((expert_count, 1, 2) + tail)
         return jnp.broadcast_to(a, (expert_count, 2, 2) + tail).reshape((slots,) + tail)
 
-    sent_rows = to_slots(own_rows, (half, WIDTH))
-    sent_stat = jnp.stack(
-        [to_slots(own_square, (half,)), to_slots(own_lead, (half,))], axis=1
-    )
-    recv_rows, recv_stat = (
-        lax.all_to_all(sent_rows, "expert", split_axis=0, concat_axis=0, tiled=True),
-        lax.all_to_all(sent_stat, "expert", split_axis=0, concat_axis=0, tiled=True),
-    )
-    stat = jnp.transpose(recv_stat, (1, 0, 2)).reshape(2, ROWS)
+    def thirds(v):
+        high = lax.reduce_precision(v, 8, 7)
+        middle = lax.reduce_precision(v - high, 8, 7)
+        return [high, middle, v - high - middle]
+
+    parts = jnp.stack(thirds(own_square) + thirds(own_lead)).astype(jnp.bfloat16)
+    parts = jnp.transpose(parts.reshape(6, 2 * expert_count, half), (1, 0, 2))
+    parts = parts.reshape(2 * expert_count, 1, 6 * half)
+    parts = jnp.pad(parts, ((0, 0), (0, 0), (0, WIDTH - 6 * half)))
+    block = jnp.concatenate([own_rows.reshape(2 * expert_count, half, WIDTH), parts], axis=1)
+    sent = to_slots(block, (half + 1, WIDTH))
+    received = lax.all_to_all(sent, "expert", split_axis=0, concat_axis=0, tiled=True)
+    recv_rows = received[:, :half]
+    stat = received[:, half, : 6 * half].astype(jnp.float32).reshape(slots, 2, 3, half)
+    stat = jnp.transpose(stat[:, :, 0] + stat[:, :, 1] + stat[:, :, 2], (1, 0, 2)).reshape(2, ROWS)
     stat = jnp.concatenate([stat, jnp.zeros((6, ROWS), jnp.float32)], axis=0)
     vmem = pl.BlockSpec(memory_space=pltpu.VMEM)
     acc, total = pl.pallas_call(

time: 137 us -> 113 us (0.82)
  blocking collectives: 0 us -> 27.5 us
  waiting for transfers between devices: 25.2 us -> 0 us
  starting transfers between devices: 14.8 us -> 0 us
  Pallas kernels: 85.8 us -> 74.9 us
    all_to_all x0 -> x1, blocking collectives: none -> 27.5 us  [on_device(): lax.all_to_all(sent, 'expert', split_axis=0, concat_axis=0, tiled=True)]
    all_to_all x2 -> x0, waiting for transfers between devices: 25.2 us -> none  [the longest x1 17.7 us: on_device(): lax.all_to_all(sent_rows, 'expert', split_axis=0, concat_axis=0, tiled=True)]
    all_to_all x2 -> x0, starting transfers between devices: 14.8 us -> none  [the longest x1 10.3 us: on_device(): lax.all_to_all(sent_stat, 'expert', split_axis=0, concat_axis=0, tiled=True)]
    pallas_call x1, Pallas kernels: 85.8 us -> 74.9 us  [on_device(): pl.pallas_call(gather_matmul, out_shape=(jax.ShapeDtypeStruct((2 * ROWS,...]
  transfers between devices with their start and end apart: 2 -> 0, of which waited for: 2 -> 0; matrix products, arithmetic and copies ran while one was open for 0% -> 0% of each run, Pallas kernels for 0% -> 0%
where the time goes in v2:
time: 113 us
  Pallas kernels  74.9 us (66%)
  blocking collectives  27.5 us (24%)
  local copies, waits for them, and re-layouts  6.2 us (5%)
  other arithmetic  3.39 us (3%)
    pallas_call x1, Pallas kernels, on_device(): pl.pallas_call(gather_matmul, out_shape=(jax.ShapeDtypeStruct((2 * ROWS,...  74.9 us
    all_to_all x1, blocking collectives, on_device(): lax.all_to_all(sent, 'expert', split_axis=0, concat_axis=0, tiled=True)  27.5 us

profile of v2, /device:TPU:1, one launch (start us, length us, event | category | flops | bytes accessed | tf_op | source)
XLA Modules:
  0.0 112.6 jit_solution(3425279066742093651)
XLA Ops:
  0.0 0.0 copy-start
  0.0 0.8 copy.53
  0.8 0.1 eq.57
  1.0 0.1 eq.53
  1.1 0.8 dynamic_slice.6
  1.9 1.0 fusion.5
  2.9 0.0 copy-done
  2.9 0.1 fusion.13
  3.0 0.7 select_reduce_fusion.2
  3.8 0.1 copy.55
  3.9 0.1 broadcast_in_dim.63
  4.0 0.1 broadcast_in_dim.57
  4.1 0.2 broadcast_in_dim.58
  4.3 0.6 reduce-window.6
  4.9 0.2 slice_reduce_fusion
  5.1 0.1 fusion.9
  5.3 0.2 select_reduce_fusion
  5.5 0.1 reduce_sum.52
  5.6 0.1 reduce_sum.55
  5.7 0.1 reshape.243
  5.8 0.1 broadcast_in_dim.56
  5.9 0.1 reshape.242
  6.0 0.3 convolution_convert_fusion
  6.3 0.1 concatenate.13
  6.3 0.1 maximum_bitcast_fusion
  6.4 0.1 broadcast_in_dim.66.clone
  6.5 0.0 copy-start.1
  6.5 27.5 %all_to_all.5 = bf16[32,21,384]{2,1,0:T(8,128)(2,1)S(1)} all-to-all(bf16[32,21,384]{2,1,0:T(8,128)(2,1)S(1)} %bitcast.29), channel_id=1, replica_groups=mesh['section'=16,'expert'=32] {'expert'}, dimensions={0} | all-to-all | bytes 1032192 | tf_op jit(solution)/shard_map/all_to_all | solution.py:242
  34.0 0.1 reshape.245.own_ref
  34.1 0.1 copy.61
  34.2 0.1 copy.62
  34.3 0.1 reshape.246
  34.4 0.0 copy-done.1
  34.4 0.0 copy-start.2
  34.5 1.4 %copy-done.2 = bf16[1,1,128,6144]{3,2,1,0:T(8,128)(2,1)S(1)} copy-done((bf16[1,1,128,6144]{3,2,1,0:T(8,128)(2,1)S(1)}, bf16[1,1,128,6144]{3,2,1,0:T(8,128)(2,1)}, u32[]{:S(2)}) %copy-start.2) | copy-done | bytes 1572888
  35.9 74.9 %shard_map.64 = (f32[1280,256]{1,0:T(8,128)S(1)}, f32[2,8,640]{2,1,0:T(8,128)S(1)}) custom-call(bf16[640,384]{1,0:T(8,128)(2,1)S(1)} %reshape.245.own_ref, f32[8,640]{1,0:T(8,128)S(1)} %concatenate.16.stat_ref, bf16[128,6144]{1,0:T(8,128)(2,1)S(1)} %bitcast.26, bf16[128,6144]{1,0:T(8,128)(2,1)S(1)} %bitcast.27), custom_call_target="tpu_custom_call" | custom-call | tf_op jit(solution)/shard_map/pallas_call | solution.py:248
  110.8 0.1 reshape.247
  110.9 0.1 rsqrt.14
  111.1 0.1 squeeze.8
  111.2 0.5 fusion.3
  111.7 0.9 copy.64
  (25 shorter events, 0.4 us)
Async XLA Ops:
  0.0 2.9 %copy-start = (bf16[6144,8]{0,1:T(8,128)(2,1)S(1)}, bf16[6144,8]{0,1:T(8,128)(2,1)}, u32[]{:S(2)}) copy-start(bf16[6144,8]{0,1:T(8,128)(2,1)} %param.9) | copy-start | bytes 294916
  6.5 28.0 %copy-start.1 = (bf16[1,1,128,6144]{3,2,1,0:T(8,128)(2,1)S(1)}, bf16[1,1,128,6144]{3,2,1,0:T(8,128)(2,1)}, u32[]{:S(2)}) copy-start(bf16[1,1,128,6144]{3,2,1,0:T(8,128)(2,1)} %param.10) | copy-start | bytes 4718596
  34.4 1.4 %copy-start.2 = (bf16[1,1,128,6144]{3,2,1,0:T(8,128)(2,1)S(1)}, bf16[1,1,128,6144]{3,2,1,0:T(8,128)(2,1)}, u32[]{:S(2)}) copy-start(bf16[1,1,128,6144]{3,2,1,0:T(8,128)(2,1)} %param.11) | copy-start | bytes 4718596

commit v3 on v2

--- a/solution.py
+++ b/solution.py
@@ -9,9 +9,10 @@
 Z = 8
 ROWS = 640
 WIDTH = 384
-SPLIT = 208
-MIDDLE = ROWS - 2 * SPLIT
-COPIES = 86
+SPLIT = 192
+AHEAD = 144
+LATE = ROWS - 2 * SPLIT - AHEAD
+COPIES = 96
 
 
 def gather_matmul(own_ref, stat_ref, gate_ref, up_ref, acc_ref, tot_ref, full, stats, send, recv, local):
@@ -65,13 +66,13 @@
         return own_ref.at[pl.ds(pl.multiple_of(lo, 16), n)]
 
     kept = (odd * (ROWS - SPLIT), SPLIT)
-    rest = ((1 - odd) * SPLIT, ROWS - SPLIT)
-    middle = (SPLIT, MIDDLE)
+    ahead = (SPLIT, AHEAD)
+    late = (SPLIT + AHEAD, LATE)
 
     def ring(kind, i, way, hop):
-        lo, n = (odd * SPLIT, SPLIT + MIDDLE) if kind == 0 else kept
+        lo, n = ((odd * SPLIT, ROWS - SPLIT), kept, ahead)[kind]
         if hop == 4:
-            first = MIDDLE if kind == 0 else SPLIT // 2 + 8
+            first = (n + 31) // 32 * 16
             lo, n = (lo, first) if way == "up" else (lo + first, n - first)
         dst = rows(mine(i) if kind == 0 else other(i), lo, n)
         start(("ring", kind, way, hop), way, own_rows(lo, n) if kind == 0 and i == 0 else dst, dst)
@@ -82,7 +83,7 @@
 
     def spread(i):
         if i:
-            dst = rows(mine(i), *middle)
+            dst = rows(mine(i), *late)
             start(("late", i), "across", dst, dst)
             dst = rows(mine(i), *kept)
             start(("y0", i), "side", dst, dst)
@@ -101,9 +102,9 @@
             dst = rows(mine(i), 0, ROWS)
             start(("p0", i), "partner", dst, dst)
             made[("late", i)].wait_recv()
-            made[("y1", i)].wait_recv()
         else:
-            made[("rest",)].wait_recv()
+            made[("late own",)].wait_recv()
+        made[("y1", i)].wait_recv()
         dst = rows(other(i), 0, ROWS)
         start(("p1", i), "partner", dst, dst)
         made[("sx", i)].wait_recv()
@@ -138,7 +139,8 @@
     ring(0, 0, "down", 1)
     ring_stat(0, "up", 1)
     ring_stat(0, "down", 1)
-    start(("rest",), "across", own_rows(*rest), rows(sec, *rest))
+    start(("ahead",), "across", own_rows(*ahead), rows(sec, *ahead))
+    start(("late own",), "across", own_rows(*late), rows(sec, *late))
     start(("p0", 0), "partner", own_ref, rows(sec, 0, ROWS))
     spread(0)
     keep = pltpu.make_async_copy(own_ref, full.at[sec, core], local.at[0])
@@ -148,6 +150,10 @@
     made[("kept",)].wait_recv()
     ring(1, 0, "up", 1)
     ring(1, 0, "down", 1)
+    spread_other(0)
+    made[("ahead",)].wait_recv()
+    ring(2, 0, "up", 1)
+    ring(2, 0, "down", 1)
     keep.wait()
     keep_stat.wait()
     ways = (("up", 0), ("down", 3))
@@ -163,6 +169,9 @@
             made[("ring", 1, way, hop)].wait_recv()
             ring(1, base + hop, way, hop + 1)
             spread_other(base + hop)
+        for way, base in ways:
+            made[("ring", 2, way, hop)].wait_recv()
+            ring(2, base + hop, way, hop + 1)
         before = [0] if hop == 1 else [hop - 1, hop + 2]
         for i in before:
             whole(i)
@@ -175,6 +184,8 @@
     for way, _ in ways:
         made[("ring", 1, way, 4)].wait_recv()
     spread_other(7)
+    for way, _ in ways:
+        made[("ring", 2, way, 4)].wait_recv()
     for i in (3, 6):
         whole(i)
     for i in (3, 6):

time: 113 us -> 112 us (level)
  no operation moved by 1% of the time
where the time goes in v3:
time: 112 us
  Pallas kernels  73.9 us (66%)
  blocking collectives  27.5 us (25%)
  local copies, waits for them, and re-layouts  6.2 us (6%)
  other arithmetic  3.39 us (3%)
    pallas_call x1, Pallas kernels, on_device(): pl.pallas_call(gather_matmul, out_shape=(jax.ShapeDtypeStruct((2 * ROWS,...  73.9 us
    all_to_all x1, blocking collectives, on_device(): lax.all_to_all(sent, 'expert', split_axis=0, concat_axis=0, tiled=True)  27.5 us

profile of v3, /device:TPU:1, one launch (start us, length us, event | category | flops | bytes accessed | tf_op | source)
XLA Modules:
  0.0 111.6 jit_solution(15323302239629077075)
XLA Ops:
  0.0 0.0 copy-start
  0.0 0.8 copy.53
  0.8 0.1 eq.57
  1.0 0.1 eq.53
  1.1 0.8 dynamic_slice.6
  1.9 1.0 fusion.5
  2.9 0.0 copy-done
  2.9 0.1 fusion.13
  3.0 0.7 select_reduce_fusion.2
  3.8 0.1 copy.55
  3.9 0.1 broadcast_in_dim.63
  4.0 0.1 broadcast_in_dim.57
  4.1 0.2 broadcast_in_dim.58
  4.3 0.6 reduce-window.6
  4.9 0.2 slice_reduce_fusion
  5.1 0.1 fusion.9
  5.3 0.2 select_reduce_fusion
  5.5 0.1 reduce_sum.52
  5.6 0.1 reduce_sum.55
  5.7 0.1 reshape.243
  5.8 0.1 broadcast_in_dim.56
  5.9 0.1 reshape.242
  6.0 0.3 convolution_convert_fusion
  6.3 0.1 concatenate.13
  6.3 0.1 maximum_bitcast_fusion
  6.4 0.1 broadcast_in_dim.66.clone
  6.5 0.0 copy-start.1
  6.5 27.5 %all_to_all.5 = bf16[32,21,384]{2,1,0:T(8,128)(2,1)S(1)} all-to-all(bf16[32,21,384]{2,1,0:T(8,128)(2,1)S(1)} %bitcast.29), channel_id=1, replica_groups=mesh['section'=16,'expert'=32] {'expert'}, dimensions={0} | all-to-all | bytes 1032192 | tf_op jit(solution)/shard_map/all_to_all | solution.py:253
  34.0 0.1 reshape.245.own_ref
  34.1 0.1 copy.61
  34.2 0.1 copy.62
  34.3 0.1 reshape.246
  34.4 0.0 copy-done.1
  34.4 0.0 copy-start.2
  34.5 1.4 %copy-done.2 = bf16[1,1,128,6144]{3,2,1,0:T(8,128)(2,1)S(1)} copy-done((bf16[1,1,128,6144]{3,2,1,0:T(8,128)(2,1)S(1)}, bf16[1,1,128,6144]{3,2,1,0:T(8,128)(2,1)}, u32[]{:S(2)}) %copy-start.2) | copy-done | bytes 1572888
  35.9 73.9 %shard_map.64 = (f32[1280,256]{1,0:T(8,128)S(1)}, f32[2,8,640]{2,1,0:T(8,128)S(1)}) custom-call(bf16[640,384]{1,0:T(8,128)(2,1)S(1)} %reshape.245.own_ref, f32[8,640]{1,0:T(8,128)S(1)} %concatenate.16.stat_ref, bf16[128,6144]{1,0:T(8,128)(2,1)S(1)} %bitcast.26, bf16[128,6144]{1,0:T(8,128)(2,1)S(1)} %bitcast.27), custom_call_target="tpu_custom_call" | custom-call | tf_op jit(solution)/shard_map/pallas_call | solution.py:259
  109.8 0.1 reshape.247
  110.0 0.1 rsqrt.14
  110.1 0.1 squeeze.8
  110.2 0.5 fusion.3
  110.7 0.9 copy.64
  (25 shorter events, 0.4 us)
Async XLA Ops:
  0.0 2.9 %copy-start = (bf16[6144,8]{0,1:T(8,128)(2,1)S(1)}, bf16[6144,8]{0,1:T(8,128)(2,1)}, u32[]{:S(2)}) copy-start(bf16[6144,8]{0,1:T(8,128)(2,1)} %param.9) | copy-start | bytes 294916
  6.5 28.0 %copy-start.1 = (bf16[1,1,128,6144]{3,2,1,0:T(8,128)(2,1)S(1)}, bf16[1,1,128,6144]{3,2,1,0:T(8,128)(2,1)}, u32[]{:S(2)}) copy-start(bf16[1,1,128,6144]{3,2,1,0:T(8,128)(2,1)} %param.10) | copy-start | bytes 4718596
  34.4 1.4 %copy-start.2 = (bf16[1,1,128,6144]{3,2,1,0:T(8,128)(2,1)S(1)}, bf16[1,1,128,6144]{3,2,1,0:T(8,128)(2,1)}, u32[]{:S(2)}) copy-start(bf16[1,1,128,6144]{3,2,1,0:T(8,128)(2,1)} %param.11) | copy-start | bytes 4718596

commit v4 on v3

--- a/solution.py
+++ b/solution.py
@@ -115,12 +115,11 @@
         cols = pl.ds(pl.multiple_of(s * WIDTH, 128), WIDTH)
         weights = jnp.concatenate([gate_ref[:, cols], up_ref[:, cols]], axis=0)
 
-        @pl.loop(0, 4)
+        @pl.loop(0, 2)
         def _(t):
-            at = pl.ds(pl.multiple_of(lax.rem(t, 2) * 320, 32), 320)
-            to = pl.ds(pl.multiple_of(t * 320, 32), 320)
+            to = pl.ds(pl.multiple_of(t * ROWS, 128), ROWS)
             part = lax.dot_general(
-                full[s, t // 2, at, :], weights, (((1,), (1,)), ((), ())),
+                full[s, t], weights, (((1,), (1,)), ((), ())),
                 preferred_element_type=jnp.float32,
             )
             if first:

time: 112 us -> 110 us (0.982)
  Pallas kernels: 73.9 us -> 72 us
    pallas_call x1, Pallas kernels: 73.9 us -> 72 us  [on_device(): pl.pallas_call(gather_matmul, out_shape=(jax.ShapeDtypeStruct((2 * ROWS,...]
where the time goes in v4:
time: 110 us
  Pallas kernels  72 us (65%)
  blocking collectives  27.5 us (25%)
  local copies, waits for them, and re-layouts  6.2 us (6%)
  other arithmetic  3.39 us (3%)
    pallas_call x1, Pallas kernels, on_device(): pl.pallas_call(gather_matmul, out_shape=(jax.ShapeDtypeStruct((2 * ROWS,...  72 us
    all_to_all x1, blocking collectives, on_device(): lax.all_to_all(sent, 'expert', split_axis=0, concat_axis=0, tiled=True)  27.5 us
    unnamed x7, local copies, waits for them, and re-layouts  2.23 us

profile of v4, /device:TPU:1, one launch (start us, length us, event | category | flops | bytes accessed | tf_op | source)
XLA Modules:
  0.0 109.7 jit_solution(16339807003854808434)
XLA Ops:
  0.0 0.0 copy-start
  0.0 0.8 copy.53
  0.8 0.1 eq.57
  1.0 0.1 eq.53
  1.1 0.8 dynamic_slice.6
  1.9 1.0 fusion.5
  2.9 0.0 copy-done
  2.9 0.1 fusion.13
  3.0 0.7 select_reduce_fusion.2
  3.8 0.1 copy.55
  3.9 0.1 broadcast_in_dim.63
  4.0 0.1 broadcast_in_dim.57
  4.1 0.2 broadcast_in_dim.58
  4.3 0.6 reduce-window.6
  4.9 0.2 slice_reduce_fusion
  5.1 0.1 fusion.9
  5.3 0.2 select_reduce_fusion
  5.5 0.1 reduce_sum.52
  5.6 0.1 reduce_sum.55
  5.7 0.1 reshape.243
  5.8 0.1 broadcast_in_dim.56
  5.9 0.1 reshape.242
  6.0 0.3 convolution_convert_fusion
  6.3 0.1 concatenate.13
  6.3 0.1 maximum_bitcast_fusion
  6.4 0.1 broadcast_in_dim.66.clone
  6.5 0.0 copy-start.1
  6.5 27.5 %all_to_all.5 = bf16[32,21,384]{2,1,0:T(8,128)(2,1)S(1)} all-to-all(bf16[32,21,384]{2,1,0:T(8,128)(2,1)S(1)} %bitcast.29), channel_id=1, replica_groups=mesh['section'=16,'expert'=32] {'expert'}, dimensions={0} | all-to-all | bytes 1032192 | tf_op jit(solution)/shard_map/all_to_all | solution.py:252
  34.0 0.1 reshape.245.own_ref
  34.1 0.1 copy.61
  34.2 0.1 copy.62
  34.3 0.1 reshape.246
  34.4 0.0 copy-done.1
  34.4 0.0 copy-start.2
  34.5 1.4 %copy-done.2 = bf16[1,1,128,6144]{3,2,1,0:T(8,128)(2,1)S(1)} copy-done((bf16[1,1,128,6144]{3,2,1,0:T(8,128)(2,1)S(1)}, bf16[1,1,128,6144]{3,2,1,0:T(8,128)(2,1)}, u32[]{:S(2)}) %copy-start.2) | copy-done | bytes 1572888
  35.9 72.0 %shard_map.64 = (f32[1280,256]{1,0:T(8,128)S(1)}, f32[2,8,640]{2,1,0:T(8,128)S(1)}) custom-call(bf16[640,384]{1,0:T(8,128)(2,1)S(1)} %reshape.245.own_ref, f32[8,640]{1,0:T(8,128)S(1)} %concatenate.16.stat_ref, bf16[128,6144]{1,0:T(8,128)(2,1)S(1)} %bitcast.26, bf16[128,6144]{1,0:T(8,128)(2,1)S(1)} %bitcast.27), custom_call_target="tpu_custom_call" | custom-call | tf_op jit(solution)/shard_map/pallas_call | solution.py:258
  107.9 0.1 reshape.247
  108.1 0.1 rsqrt.14
  108.2 0.1 squeeze.8
  108.3 0.5 fusion.3
  108.9 0.9 copy.64
  (25 shorter events, 0.4 us)
Async XLA Ops:
  0.0 2.9 %copy-start = (bf16[6144,8]{0,1:T(8,128)(2,1)S(1)}, bf16[6144,8]{0,1:T(8,128)(2,1)}, u32[]{:S(2)}) copy-start(bf16[6144,8]{0,1:T(8,128)(2,1)} %param.9) | copy-start | bytes 294916
  6.5 28.0 %copy-start.1 = (bf16[1,1,128,6144]{3,2,1,0:T(8,128)(2,1)S(1)}, bf16[1,1,128,6144]{3,2,1,0:T(8,128)(2,1)}, u32[]{:S(2)}) copy-start(bf16[1,1,128,6144]{3,2,1,0:T(8,128)(2,1)} %param.10) | copy-start | bytes 4718596
  34.4 1.4 %copy-start.2 = (bf16[1,1,128,6144]{3,2,1,0:T(8,128)(2,1)S(1)}, bf16[1,1,128,6144]{3,2,1,0:T(8,128)(2,1)}, u32[]{:S(2)}) copy-start(bf16[1,1,128,6144]{3,2,1,0:T(8,128)(2,1)} %param.11) | copy-start | bytes 4718596
